TPU v7x, 128 devices: a whole 4x4x4 slice. The times are simulated.
128 devices in a mesh: grp: 8 (over y, core), dev: 16 (over x, z).
Axes of the slice: x: 4, y: 4, z: 4, core: 2. Of those that a mesh axis runs over, the one named last changes fastest.
Arguments:
- suffix_queries: bfloat16 [16384, 2048], P(('grp', 'dev')), may hold values from -12 to 12
- suffix_keys: bfloat16 [16384, 2048], P(('grp', 'dev')), may hold values from -12 to 12
- suffix_values: bfloat16 [16384, 2048], P(('grp', 'dev')), may hold values from -6 to 6
- layer_input: bfloat16 [16384, 2048], P(('grp', 'dev')), may hold values from -6 to 6
- suffix_lengths: int32 [128, 8], P(('grp', 'dev')), may hold values from 1 to 32, as said below
- request_group: int32 [128, 8], P(('grp', 'dev')), may hold values from 0 to 7, as said below
- prefix_keys: bfloat16 [8, 4096, 2048], P('grp', None, 'dev'), may hold values from -12 to 12
- prefix_values: bfloat16 [8, 4096, 2048], P('grp', None, 'dev'), may hold values from -6 to 6
- up_weight: bfloat16 [2048, 8192], P(None, ('grp', 'dev')), may hold values from -0.125 to 0.125
- up_bias: bfloat16 [8192], P(('grp', 'dev')), may hold values from -3 to 3
- down_weight: bfloat16 [8192, 2048], P(('grp', 'dev')), may hold values from -0.0625 to 0.0625
- down_bias: float32 [2048], replicated, may hold values from -3 to 3
- attn_gain: float32 [2048], replicated, may hold values from 0.5 to 1.5
- attn_shift: float32 [2048], replicated, may hold values from -2 to 2
- out_gain: float32 [2048], replicated, may hold values from 0.5 to 1.5
- out_shift: float32 [2048], replicated, may hold values from -2 to 2
Outputs:
- layer_output: bfloat16 [16384, 2048], P(('grp', 'dev'))
Inputs may be any that keep to these rules, and one draw needn't show every extreme that they name: `suffix_lengths`: each row lists one device's 8 requests in slot order; they fill its 128 slots exactly, and at least one of them has 32 tokens. `request_group`: the 8 requests of one row name every prefix exactly once.
All inputs are finite; a program needn't handle non-finite values.
Results may differ from a plain program's by a relative error of at most 0.014.
Values may be sent and summed in bfloat16 or wider, within the bound.
A program may use at most 128 MiB of HBM per device.

v0:
```python
import math
import jax
import jax.numpy as jnp
from jax import lax
from jax.sharding import PartitionSpec as P

HD = 128
norm_eps = 1e-12


def layer_norm(summed, norm_gain, norm_shift):
    row_mean = jnp.mean(summed, axis=-1, keepdims=True)
    centred = summed - row_mean
    spread = jnp.mean(centred * centred, axis=-1, keepdims=True)
    return centred * lax.rsqrt(spread + norm_eps) * norm_gain + norm_shift


def request_layout(lengths, slot_count):
    end_points = jnp.cumsum(lengths)
    starts = end_points - lengths
    positions = lax.iota(jnp.int32, slot_count)
    member = (positions[:, None] >= starts[None, :]) & (positions[:, None] < end_points[None, :])
    slot_ids = lax.iota(jnp.int32, lengths.shape[0])
    segment = jnp.sum(jnp.where(member, slot_ids[None, :], 0), axis=1)
    return (starts, segment)


def expand_rows(piece_rows, up_matrix, up_offset):
    product = jnp.dot(piece_rows, up_matrix, preferred_element_type=jnp.float32)
    return jax.nn.gelu(product + up_offset.astype(jnp.float32), approximate=True).astype(
        jnp.bfloat16
    )


def attend_prefix(arrived, cache_keys, cache_values):
    sources, row_count, part_width = arrived.shape
    local_heads = part_width // HD
    per_block = math.gcd(sources, max(1, 512 // row_count))
    query_blocks = arrived.reshape(sources // per_block, per_block * row_count, local_heads, HD)
    key_heads = cache_keys.reshape(-1, local_heads, HD)
    value_heads = cache_values.reshape(-1, local_heads, HD)

    def one_block(query_block):
        scores = jnp.einsum(
            "qhd,khd->hqk", query_block, key_heads, preferred_element_type=jnp.float32
        ) * HD ** (-0.5)
        row_top = jnp.max(scores, axis=2).astype(jnp.bfloat16)
        weights = jnp.exp(
            scores - lax.optimization_barrier(row_top).astype(jnp.float32)[:, :, None]
        )
        row_sum = jnp.sum(weights, axis=2)
        mixed_sum = jnp.einsum(
            "hqk,khd->qhd",
            weights.astype(jnp.bfloat16),
            value_heads,
            preferred_element_type=jnp.float32,
        )
        answer = (mixed_sum / row_sum.T[:, :, None]).astype(jnp.bfloat16)
        return (answer.reshape(-1, part_width), row_top.T, row_sum.T.astype(jnp.bfloat16))

    answer, row_top, row_sum = lax.map(one_block, query_blocks)
    return (
        answer.reshape(sources, row_count, part_width),
        row_top.reshape(sources, row_count, local_heads),
        row_sum.reshape(sources, row_count, local_heads),
    )


def attend_suffix(query_rows, key_rows, value_rows, segment, head_count):
    slot_count = query_rows.shape[0]
    query_heads = query_rows.reshape(slot_count, head_count, HD)
    key_heads = key_rows.reshape(slot_count, head_count, HD)
    value_heads = value_rows.reshape(slot_count, head_count, HD)
    scores = jnp.einsum(
        "qhd,khd->hqk", query_heads, key_heads, preferred_element_type=jnp.float32
    ) * HD ** (-0.5)
    positions = lax.iota(jnp.int32, slot_count)
    visible = ((segment[:, None] == segment[None, :]) & (positions[None, :] <= positions[:, None]))[
        None
    ]
    row_top = jnp.max(jnp.where(visible, scores, -jnp.inf), axis=2)
    weights = jnp.where(visible, jnp.exp(scores - row_top[:, :, None]), 0.0)
    row_sum = jnp.sum(weights, axis=2)
    mixed_sum = jnp.einsum(
        "hqk,khd->qhd",
        weights.astype(jnp.bfloat16),
        value_heads,
        preferred_element_type=jnp.float32,
    )
    return (row_top.T, row_sum.T, mixed_sum)


def merge_parts(far_answer, far_top, far_sum, own_top, own_sum, own_mixed):
    far_top = far_top.astype(jnp.float32)
    far_sum = far_sum.astype(jnp.float32)
    joint_top = jnp.maximum(far_top, own_top)
    far_weight = jnp.exp(far_top - joint_top) * far_sum
    own_weight = jnp.exp(own_top - joint_top)
    numerator = (
        far_weight[:, :, None] * far_answer.astype(jnp.float32) + own_weight[:, :, None] * own_mixed
    )
    return numerator / (far_weight + own_weight * own_sum)[:, :, None]


def on_device(
    suffix_queries,
    suffix_keys,
    suffix_values,
    layer_input,
    suffix_lengths,
    request_group,
    prefix_keys,
    prefix_values,
    up_weight,
    up_bias,
    down_weight,
    down_bias,
    attn_gain,
    attn_shift,
    out_gain,
    out_shift,
):
    slot_count, model_width = suffix_queries.shape
    head_count = model_width // HD
    group_count = lax.axis_size("grp")
    column_count = lax.axis_size("dev")
    part_width = model_width // column_count
    local_heads = part_width // HD
    capacity = 2 * slot_count // group_count
    lengths = suffix_lengths[0]
    groups = request_group[0]
    request_total = lengths.shape[0]
    starts, segment = request_layout(lengths, slot_count)
    anchor = jnp.zeros((), jnp.int32)
    padded = jnp.concatenate(
        [suffix_queries, jnp.zeros((capacity, model_width), jnp.bfloat16)], axis=0
    )
    slot_rank = lax.iota(jnp.int32, capacity)
    outgoing = jnp.zeros((group_count, column_count, capacity, part_width), jnp.bfloat16)
    for request in range(request_total):
        taken = lax.dynamic_slice_in_dim(padded, starts[request], capacity, 0)
        taken = jnp.where((slot_rank < lengths[request])[:, None], taken, jnp.zeros_like(taken))
        split_rows = taken.reshape(capacity, column_count, part_width).transpose(1, 0, 2)
        outgoing = lax.dynamic_update_slice(
            outgoing, split_rows[None], (groups[request], anchor, anchor, anchor)
        )
    cache_keys = prefix_keys[0]
    cache_values = prefix_values[0]
    answer_part, top_part, sum_part = attend_prefix(
        lax.all_to_all(
            outgoing.reshape(group_count * column_count, capacity, part_width),
            ("grp", "dev"),
            split_axis=0,
            concat_axis=0,
            tiled=True,
        ),
        cache_keys,
        cache_values,
    )
    answer = lax.all_to_all(answer_part, ("grp", "dev"), split_axis=0, concat_axis=0, tiled=True)
    far_top = lax.all_to_all(top_part, ("grp", "dev"), split_axis=0, concat_axis=0, tiled=True)
    far_sum = lax.all_to_all(sum_part, ("grp", "dev"), split_axis=0, concat_axis=0, tiled=True)
    answer = answer.reshape(group_count, column_count, capacity, part_width)
    far_top = far_top.reshape(group_count, column_count, capacity, local_heads)
    far_sum = far_sum.reshape(group_count, column_count, capacity, local_heads)
    placed_answer = jnp.zeros((slot_count + capacity, model_width), jnp.bfloat16)
    placed_top = jnp.zeros((slot_count + capacity, head_count), jnp.bfloat16)
    placed_sum = jnp.zeros((slot_count + capacity, head_count), jnp.bfloat16)
    for request in range(request_total):
        own_answer = (
            lax.dynamic_index_in_dim(answer, groups[request], 0, keepdims=False)
            .transpose(1, 0, 2)
            .reshape(capacity, model_width)
        )
        own_top_rows = (
            lax.dynamic_index_in_dim(far_top, groups[request], 0, keepdims=False)
            .transpose(1, 0, 2)
            .reshape(capacity, head_count)
        )
        own_sum_rows = (
            lax.dynamic_index_in_dim(far_sum, groups[request], 0, keepdims=False)
            .transpose(1, 0, 2)
            .reshape(capacity, head_count)
        )
        placed_answer = lax.dynamic_update_slice(
            placed_answer, own_answer, (starts[request], anchor)
        )
        placed_top = lax.dynamic_update_slice(placed_top, own_top_rows, (starts[request], anchor))
        placed_sum = lax.dynamic_update_slice(placed_sum, own_sum_rows, (starts[request], anchor))
    own_top, own_sum, own_mixed = attend_suffix(
        suffix_queries, suffix_keys, suffix_values, segment, head_count
    )
    far_rows = placed_answer[:slot_count].reshape(slot_count, head_count, HD)
    context = merge_parts(
        far_rows, placed_top[:slot_count], placed_sum[:slot_count], own_top, own_sum, own_mixed
    )
    hidden_state = layer_norm(
        layer_input.astype(jnp.float32) + context.reshape(slot_count, model_width),
        attn_gain,
        attn_shift,
    ).astype(jnp.bfloat16)
    up_slice, bias_slice, down_slice = (
        lax.all_gather(up_weight, "grp", axis=1, tiled=True),
        lax.all_gather(up_bias, "grp", axis=0, tiled=True),
        lax.all_gather(down_weight, "grp", axis=0, tiled=True),
    )
    activation = expand_rows(
        lax.all_gather(hidden_state, "dev", axis=0, tiled=True), up_slice, bias_slice
    )
    mlp_sum = lax.psum_scatter(
        jnp.dot(activation, down_slice, preferred_element_type=jnp.float32).astype(jnp.bfloat16),
        "dev",
        scatter_dimension=0,
        tiled=True,
    ).astype(jnp.float32)
    return layer_norm(
        hidden_state.astype(jnp.float32) + mlp_sum + down_bias, out_gain, out_shift
    ).astype(jnp.bfloat16)


def solution(mesh):
    placed = (
        P(("grp", "dev"), None),
        P(("grp", "dev"), None),
        P(("grp", "dev"), None),
        P(("grp", "dev"), None),
        P(("grp", "dev"), None),
        P(("grp", "dev"), None),
        P("grp", None, "dev"),
        P("grp", None, "dev"),
        P(None, ("grp", "dev")),
        P(("grp", "dev")),
        P(("grp", "dev"), None),
        P(),
        P(),
        P(),
        P(),
        P(),
    )
    return jax.shard_map(
        on_device, mesh=mesh, in_specs=placed, out_specs=P(("grp", "dev"), None), check_vma=False
    )
```

profile of v0, /device:TPU:0, one launch (start us, length us, event | category | flops | bytes accessed | tf_op | source)
XLA Modules:
  0.0 412.4 jit_solution(14731411691771604662)
XLA Ops:
  57.2 11.2 %all-to-all-start = ((bf16[128,32,128]{2,1,0:T(8,128)(2,1)}), bf16[128,32,128]{2,1,0:T(8,128)(2,1)S(1)}, u32[]{:S(2)}, u32[]{:S(2)}) async-start(bf16[128,32,128]{2,1,0:T(8,128)(2,1)} %bitcast.51), calls=%async_computation | async-start | bytes 2097152 | tf_op jit(solution)/shard_map/all_to_all | solution.py:150
  69.2 18.3 %all-to-all-done = bf16[128,32,128]{2,1,0:T(8,128)(2,1)S(1)} async-done(((bf16[128,32,128]{2,1,0:T(8,128)(2,1)}), bf16[128,32,128]{2,1,0:T(8,128)(2,1)S(1)}, u32[]{:S(2)}, u32[]{:S(2)}) %all-to-all-start) | async-done | bytes 1048608 | tf_op jit(solution)/shard_map/all_to_all | solution.py:150
  87.5 41.1 %while.14 = (s32[]{:T(128)}, bf16[8,512,128]{2,1,0:T(8,128)(2,1)}, bf16[8,512,1]{1,0,2:T(8,128)(2,1)S(1)}, bf16[8,512,1]{1,0,2:T(8,128)(2,1)S(1)}, bf16[8,512,1,...) while((s32[]{:T(128)}, bf16[8,512,128]{2,1,0:T(8,128)(2,1)}, ...), condition=%wide.region_4.5_spmd, body=%wide.region_1.4_spmd.sunk | while | flops 1090650112 | bytes 31745168 | solution.py:61
  126.3 2.2 fusion.119
  129.3 4.6 %all-to-all-start.2 = ((bf16[128,32,1]{1,2,0:T(2,128)(2,1)}), bf16[128,32,1]{1,2,0:T(2,128)(2,1)S(1)}, u32[]{:S(2)}, u32[]{:S(2)}) async-start(bf16[128,32,1]{1,2,0:T(2,128)(2,1)} %reshape.401), calls=%async_computation.2 | async-start | bytes 131072 | tf_op jit(solution)/shard_map/all_to_all | solution.py:162
  134.6 8.8 %all-to-all-done.2 = bf16[128,32,1]{1,2,0:T(2,128)(2,1)S(1)} async-done(((bf16[128,32,1]{1,2,0:T(2,128)(2,1)}), bf16[128,32,1]{1,2,0:T(2,128)(2,1)S(1)}, u32[]{:S(2)}, u32[]{:S(2)}) %all-to-all-start.2) | async-done | bytes 8224 | tf_op jit(solution)/shard_map/all_to_all | solution.py:162
  143.4 4.6 %all-to-all-start.1 = ((bf16[128,32,1]{1,2,0:T(2,128)(2,1)}), bf16[128,32,1]{1,2,0:T(2,128)(2,1)S(1)}, u32[]{:S(2)}, u32[]{:S(2)}) async-start(bf16[128,32,1]{1,2,0:T(2,128)(2,1)} %reshape.400), calls=%async_computation.1 | async-start | bytes 131072 | tf_op jit(solution)/shard_map/all_to_all | solution.py:161
  148.0 9.4 %all-to-all-done.1 = bf16[128,32,1]{1,2,0:T(2,128)(2,1)S(1)} async-done(((bf16[128,32,1]{1,2,0:T(2,128)(2,1)}), bf16[128,32,1]{1,2,0:T(2,128)(2,1)S(1)}, u32[]{:S(2)}, u32[]{:S(2)}) %all-to-all-start.1) | async-done | bytes 8224 | tf_op jit(solution)/shard_map/all_to_all | solution.py:161
  157.4 4.6 %all-to-all-start.3 = ((bf16[128,32,128]{2,1,0:T(8,128)(2,1)}), bf16[128,32,128]{2,1,0:T(8,128)(2,1)S(1)}, u32[]{:S(2)}, u32[]{:S(2)}) async-start(bf16[128,32,128]{2,1,0:T(8,128)(2,1)} %bitcast.380), calls=%async_computation.3 | async-start | bytes 2097152 | tf_op jit(solution)/shard_map/all_to_all | solution.py:160
  170.3 10.7 %all-to-all-done.3 = bf16[128,32,128]{2,1,0:T(8,128)(2,1)S(1)} async-done(((bf16[128,32,128]{2,1,0:T(8,128)(2,1)}), bf16[128,32,128]{2,1,0:T(8,128)(2,1)S(1)}, u32[]{:S(2)}, u32[]{:S(2)}) %all-to-all-start.3) | async-done | bytes 1048608 | tf_op jit(solution)/shard_map/all_to_all | solution.py:160
  187.3 4.9 %dynamic_update_slice.131 = bf16[160,2048]{0,1:T(8,128)(2,1)S(1)} dynamic-update-slice(bf16[160,2048]{0,1:T(8,128)(2,1)S(1)} %broadcast_in_dim.168, bf16[32,2048]{0,1:T(8,128)(2,1)} %bitcast.379, s32[]{:T(128)S(6)} %select_n.134, s32[]{:T(128)} %constant.96.clone.1) | dynamic-update-slice | bytes 262148 | tf_op jit(solution)/shard_map/dynamic_update_slice | solution.py:185
  192.2 5.9 %dynamic_update_slice.132 = bf16[160,2048]{0,1:T(8,128)(2,1)S(1)} dynamic-update-slice(bf16[160,2048]{0,1:T(8,128)(2,1)S(1)} %dynamic_update_slice.131, bf16[32,2048]{0,1:T(8,128)(2,1)} %bitcast.378, s32[]{:T(128)S(6)} %select_n.137, s32[]{:T(128)} %constant.96.clone.1) | dynamic-update-slice | bytes 262148 | tf_op jit(solution)/shard_map/dynamic_update_slice | solution.py:185
  198.1 5.9 %dynamic_update_slice.133 = bf16[160,2048]{0,1:T(8,128)(2,1)S(1)} dynamic-update-slice(bf16[160,2048]{0,1:T(8,128)(2,1)S(1)} %dynamic_update_slice.132, bf16[32,2048]{0,1:T(8,128)(2,1)} %bitcast.377, s32[]{:T(128)S(6)} %select_n.140, s32[]{:T(128)} %constant.96.clone.1) | dynamic-update-slice | bytes 262148 | tf_op jit(solution)/shard_map/dynamic_update_slice | solution.py:185
  204.1 5.9 %dynamic_update_slice.134 = bf16[160,2048]{0,1:T(8,128)(2,1)S(1)} dynamic-update-slice(bf16[160,2048]{0,1:T(8,128)(2,1)S(1)} %dynamic_update_slice.133, bf16[32,2048]{0,1:T(8,128)(2,1)} %bitcast.376, s32[]{:T(128)S(6)} %select_n.143, s32[]{:T(128)} %constant.96.clone.1) | dynamic-update-slice | bytes 262148 | tf_op jit(solution)/shard_map/dynamic_update_slice | solution.py:185
  210.0 5.9 %dynamic_update_slice.135 = bf16[160,2048]{0,1:T(8,128)(2,1)S(1)} dynamic-update-slice(bf16[160,2048]{0,1:T(8,128)(2,1)S(1)} %dynamic_update_slice.134, bf16[32,2048]{0,1:T(8,128)(2,1)} %bitcast.375, s32[]{:T(128)S(6)} %select_n.146, s32[]{:T(128)} %constant.96.clone.1) | dynamic-update-slice | bytes 262148 | tf_op jit(solution)/shard_map/dynamic_update_slice | solution.py:185
  216.0 4.0 dynamic_update_slice.136
  220.0 4.0 dynamic_update_slice.137
  224.0 4.2 %dynamic_update_slice.138 = bf16[160,2048]{0,1:T(8,128)(2,1)S(1)} dynamic-update-slice(bf16[160,2048]{0,1:T(8,128)(2,1)S(1)} %dynamic_update_slice.137, bf16[32,2048]{0,1:T(8,128)(2,1)S(1)} %bitcast.372, s32[]{:T(128)S(6)} %select_n.155, s32[]{:T(128)} %constant.96.clone.1) | dynamic-update-slice | bytes 262148 | tf_op jit(solution)/shard_map/dynamic_update_slice | solution.py:185
  228.3 2.8 fusion.36
  235.9 12.8 %all-reduce.1 = bf16[512]{0:T(512)(128)(2,1)S(1)} all-reduce(bf16[512]{0:T(512)(128)(2,1)S(1)} %dynamic-update-slice), channel_id=1, replica_groups=mesh['grp'=8,'dev'=16] {'grp'}, use_global_device_ids=true, to_apply=%add.1 | all-reduce | flops 512 | bytes 2048
  248.8 52.0 %all-gather.4.cloned.1.call-done = bf16[2048,2048]{1,0:T(8,128)(2,1)} async-done(((bf16[128,2048]{1,0:T(8,128)(2,1)}), bf16[2048,2048]{1,0:T(8,128)(2,1)}) %all-gather.4.cloned.1.call-update) | async-done | bytes 8388624 | tf_op jit(solution)/shard_map/all_gather | solution.py:208
  300.8 15.2 %convolution_convert_fusion = bf16[2048,2048]{1,0:T(8,128)(2,1)} fusion(bf16[512,2048]{1,0:T(8,128)(2,1)} %all-gather.8.cloned.1.call-done, bf16[2048,2048]{1,0:T(8,128)(2,1)} %all-gather.4.cloned.1.call-done, bf16[2048,512]{0,1:T(8,128)(2,1)} %all-gather.6.cloned.1.call-done, f32[512]{0:T(512)S(1)} %convert_element_type.97), kind=kOutput, calls=%fused_computation.17 | convolution fusion | flops 8604614656 | bytes 20973568 | tf_op jit(solution)/shard_map/dot_general | solution.py:211
  316.1 84.9 %reduce-scatter.2.cloned.1.call-done = bf16[128,2048]{1,0:T(8,128)(2,1)} async-done(((bf16[2048,2048]{1,0:T(8,128)(2,1)}), bf16[128,2048]{1,0:T(8,128)(2,1)}) %reduce-scatter.2.cloned.1.call-update) | async-done | bytes 524304 | tf_op jit(solution)/shard_map/reduce_scatter | solution.py:210
  403.7 2.2 add_convert_fusion
  (215 shorter events, 82.7 us)
Async XLA Ops:
  6.5 157.7 %copy-start = (bf16[128,2048]{1,0:T(8,128)(2,1)S(1)}, bf16[128,2048]{1,0:T(8,128)(2,1)}, u32[]{:S(2)}) copy-start(bf16[128,2048]{1,0:T(8,128)(2,1)} %param.19) | copy-start | bytes 1572868
  6.5 80.9 %copy-start.1 = (bf16[1,4096,128]{2,1,0:T(8,128)(2,1)S(1)}, bf16[1,4096,128]{2,1,0:T(8,128)(2,1)}, u32[]{:S(2)}) copy-start(bf16[1,4096,128]{2,1,0:T(8,128)(2,1)} %param.24) | copy-start | bytes 3145732
  6.5 242.2 %all-gather.6.cloned.1.call-start = ((), (), s32[]{:S(2)}) async-start(), calls=%async_computation.6 | async-start | bytes 2359296 | tf_op jit(solution)/shard_map/all_gather | solution.py:203
  57.2 30.3 %all-to-all-start = ((bf16[128,32,128]{2,1,0:T(8,128)(2,1)}), bf16[128,32,128]{2,1,0:T(8,128)(2,1)S(1)}, u32[]{:S(2)}, u32[]{:S(2)}) async-start(bf16[128,32,128]{2,1,0:T(8,128)(2,1)} %bitcast.51), calls=%async_computation | async-start | bytes 2097152 | tf_op jit(solution)/shard_map/all_to_all | solution.py:150
  68.4 180.4 %all-gather.8.cloned.1.call-start = ((), (), s32[]{:S(2)}) async-start(), calls=%async_computation.7 | async-start | bytes 2359296 | tf_op jit(solution)/shard_map/all_gather | solution.py:205
  87.5 60.5 %copy-start.7 = (s32[1,8]{1,0:T(1,128)S(1)}, s32[1,8]{1,0:T(1,128)}, u32[]{:S(2)}) copy-start(s32[1,8]{1,0:T(1,128)} %param.22) | copy-start | bytes 100
  87.5 76.8 %copy-start.4 = (bf16[128,2048]{1,0:T(8,128)(2,1)S(1)}, bf16[128,2048]{1,0:T(8,128)(2,1)}, u32[]{:S(2)}) copy-start(bf16[128,2048]{1,0:T(8,128)(2,1)} %param.18) | copy-start | bytes 1572868
  94.0 1.5 copy-start.12
  99.1 1.5 copy-start.12
  104.3 1.5 copy-start.12
  129.3 14.0 %all-to-all-start.2 = ((bf16[128,32,1]{1,2,0:T(2,128)(2,1)}), bf16[128,32,1]{1,2,0:T(2,128)(2,1)S(1)}, u32[]{:S(2)}, u32[]{:S(2)}) async-start(bf16[128,32,1]{1,2,0:T(2,128)(2,1)} %reshape.401), calls=%async_computation.2 | async-start | bytes 131072 | tf_op jit(solution)/shard_map/all_to_all | solution.py:162
  143.4 14.0 %all-to-all-start.1 = ((bf16[128,32,1]{1,2,0:T(2,128)(2,1)}), bf16[128,32,1]{1,2,0:T(2,128)(2,1)S(1)}, u32[]{:S(2)}, u32[]{:S(2)}) async-start(bf16[128,32,1]{1,2,0:T(2,128)(2,1)} %reshape.400), calls=%async_computation.1 | async-start | bytes 131072 | tf_op jit(solution)/shard_map/all_to_all | solution.py:161
  157.4 23.7 %all-to-all-start.3 = ((bf16[128,32,128]{2,1,0:T(8,128)(2,1)}), bf16[128,32,128]{2,1,0:T(8,128)(2,1)S(1)}, u32[]{:S(2)}, u32[]{:S(2)}) async-start(bf16[128,32,128]{2,1,0:T(8,128)(2,1)} %bitcast.380), calls=%async_computation.3 | async-start | bytes 2097152 | tf_op jit(solution)/shard_map/all_to_all | solution.py:160
  162.0 138.8 %all-gather.4.cloned.1.call-start = ((), (), s32[]{:S(2)}) async-start(), calls=%async_computation.5 | async-start | bytes 8912896 | tf_op jit(solution)/shard_map/all_gather | solution.py:208
  228.3 4.4 %copy-start.3 = (bf16[128,2048]{1,0:T(8,128)(2,1)S(1)}, bf16[128,2048]{1,0:T(8,128)(2,1)}, u32[]{:S(2)}) copy-start(bf16[128,2048]{1,0:T(8,128)(2,1)} %param.21) | copy-start | bytes 1572868
  228.3 4.9 %copy-start.8 = (f32[2048]{0:T(1024)S(1)}, f32[2048]{0:T(1024)}, u32[]{:S(2)}) copy-start(f32[2048]{0:T(1024)} %param.31) | copy-start | bytes 24580
  228.3 4.9 %copy-start.9 = (f32[2048]{0:T(1024)S(1)}, f32[2048]{0:T(1024)}, u32[]{:S(2)}) copy-start(f32[2048]{0:T(1024)} %param.30) | copy-start | bytes 24580
  231.1 3.3 copy-start.14
  231.1 4.5 %copy-start.13 = (bf16[64]{0:T(256)(128)(2,1)S(1)}, bf16[64]{0:T(256)(128)(2,1)}, u32[]{:S(2)}) copy-start(bf16[64]{0:T(256)(128)(2,1)} %param.27) | copy-start | bytes 388
  234.3 166.6 %reduce-scatter.2.cloned.1.call-start = ((), (), s32[]{:S(2)}) async-start(), calls=%async_computation.8 | async-start | bytes 8912896 | tf_op jit(solution)/shard_map/reduce_scatter | solution.py:210
  316.0 84.9 %copy-start.2 = (bf16[128,2048]{1,0:T(8,128)(2,1)S(1)}, bf16[128,2048]{1,0:T(8,128)(2,1)}, u32[]{:S(2)}) copy-start(bf16[128,2048]{1,0:T(8,128)(2,1)} %add_convert_fusion.1) | copy-start | bytes 1572868
  316.0 84.9 %copy-start.6 = (f32[2048]{0:T(1024)S(1)}, f32[2048]{0:T(1024)}, u32[]{:S(2)}) copy-start(f32[2048]{0:T(1024)} %param.29) | copy-start | bytes 24580
  316.0 87.6 %copy-start.10 = (f32[2048]{0:T(1024)S(1)}, f32[2048]{0:T(1024)}, u32[]{:S(2)}) copy-start(f32[2048]{0:T(1024)} %param.33) | copy-start | bytes 24580
  316.0 87.6 %copy-start.11 = (f32[2048]{0:T(1024)S(1)}, f32[2048]{0:T(1024)}, u32[]{:S(2)}) copy-start(f32[2048]{0:T(1024)} %param.32) | copy-start | bytes 24580
  (6 other events, 8.6 us)
Sparse Core Ops, SparseCore 0:
  9.1 27.6 all-gather.5
  71.0 26.2 all-gather.7
  234.5 66.3 all-gather.3
  316.2 84.7 reduce-scatter.1
where the time goes:
time: 414 us; the launch traced here: 412 us
  waiting for transfers between devices  186 us (45%)
  local copies, waits for them, and re-layouts  69.7 us (17%)
  matrix products  46.3 us (11%)
  between operations  44.2 us (11%)
  other arithmetic  28.4 us (7%)
  starting transfers between devices  25.1 us (6%)
  blocking collectives  12.8 us (3%)
    reduce_scatter x1, waiting for transfers between devices, on_device(): lax.psum_scatter(jnp.dot(activation, down_slice, preferred_element_type=j...  84.9 us
    all_gather x1, waiting for transfers between devices, on_device(): lax.all_gather(hidden_state, 'dev', axis=0, tiled=True)  52 us
    dynamic_update_slice x8, local copies, waits for them, and re-layouts, on_device(): lax.dynamic_update_slice(placed_answer, own_answer, (starts[request], anc...  40.9 us
    all_to_all x1, waiting for transfers between devices, on_device(): lax.all_to_all(outgoing.reshape(group_count * column_count, capacity, par...  18.3 us
    dot_general x8, matrix products, one_block(): jnp.einsum('hqk,khd->qhd', weights.astype(jnp.bfloat16), value_heads, pre...  17.2 us
    dot_general x1, matrix products, on_device(): jnp.dot(activation, down_slice, preferred_element_type=jnp.float32)  15.2 us
    unnamed x1, blocking collectives  12.8 us
    reduce_sum x8, other arithmetic, one_block(): row_sum = jnp.sum(weights, axis=2)  12 us
  transfers between devices with their start and end apart: 8, of which 6 were waited for; matrix products, arithmetic and copies ran while one was open for 30% of the time, Pallas kernels for 0%

commit v1 on v0

--- a/solution.py
+++ b/solution.py
@@ -205,7 +205,11 @@
         lax.all_gather(down_weight, "grp", axis=0, tiled=True),
     )
     activation = expand_rows(
-        lax.all_gather(hidden_state, "dev", axis=0, tiled=True), up_slice, bias_slice
+        jnp.concatenate(
+            lax.all_to_all(jnp.stack([hidden_state] * lax.axis_size("dev")), "dev", 0, 0), axis=0
+        ),
+        up_slice,
+        bias_slice,
     )
     mlp_sum = lax.psum_scatter(
         jnp.dot(activation, down_slice, preferred_element_type=jnp.float32).astype(jnp.bfloat16),

time: 414 us -> 504 us (1.22)
  waiting for transfers between devices: 186 us -> 266 us
  starting transfers between devices: 25.1 us -> 30.2 us
    all_to_all x0 -> x1, waiting for transfers between devices: none -> 85.8 us  [on_device(): lax.all_to_all(jnp.stack([hidden_state] * lax.axis_size('dev')), 'dev', 0...]
    all_gather x1 -> x0, waiting for transfers between devices: 52 us -> none  [on_device(): lax.all_gather(hidden_state, 'dev', axis=0, tiled=True)]
    all_gather x1, waiting for transfers between devices: 0.02 us -> 27.4 us  [on_device(): lax.all_gather(down_weight, 'grp', axis=0, tiled=True)]
    all_gather x1, waiting for transfers between devices: 0.01 us -> 11 us  [on_device(): lax.all_gather(up_weight, 'grp', axis=1, tiled=True)]
    reduce_scatter x1, waiting for transfers between devices: 84.9 us -> 92.4 us  [on_device(): lax.psum_scatter(jnp.dot(activation, down_slice, preferred_element_type=j...]
  transfers between devices with their start and end apart: 8 -> 8, of which waited for: 6 -> 8; matrix products, arithmetic and copies ran while one was open for 30% -> 2% of each run, Pallas kernels for 0% -> 0%
where the time goes in v1:
time: 504 us; the launch traced here: 502 us
  waiting for transfers between devices  266 us (53%)
  local copies, waits for them, and re-layouts  73.7 us (15%)
  matrix products  46.4 us (9%)
  between operations  44.3 us (9%)
  starting transfers between devices  30.2 us (6%)
  other arithmetic  27.7 us (5%)
  blocking collectives  13.2 us (3%)
    reduce_scatter x1, waiting for transfers between devices, on_device(): lax.psum_scatter(jnp.dot(activation, down_slice, preferred_element_type=j...  92.4 us
    all_to_all x1, waiting for transfers between devices, on_device(): lax.all_to_all(jnp.stack([hidden_state] * lax.axis_size('dev')), 'dev', 0...  85.8 us
    dynamic_update_slice x8, local copies, waits for them, and re-layouts, on_device(): lax.dynamic_update_slice(placed_answer, own_answer, (starts[request], anc...  40.9 us
    all_gather x1, waiting for transfers between devices, on_device(): lax.all_gather(down_weight, 'grp', axis=0, tiled=True)  27.4 us
    all_to_all x1, waiting for transfers between devices, on_device(): lax.all_to_all(outgoing.reshape(group_count * column_count, capacity, par...  19 us
    dot_general x8, matrix products, one_block(): jnp.einsum('hqk,khd->qhd', weights.astype(jnp.bfloat16), value_heads, pre...  17.2 us
    dot_general x1, matrix products, on_device(): jnp.dot(activation, down_slice, preferred_element_type=jnp.float32)  15.2 us
    unnamed x1, blocking collectives  13.2 us
  transfers between devices with their start and end apart: 8, of which 8 were waited for; matrix products, arithmetic and copies ran while one was open for 2% of the time, Pallas kernels for 0%

profile of v1, /device:TPU:0, one launch (start us, length us, event | category | flops | bytes accessed | tf_op | source)
XLA Modules:
  0.0 501.9 jit_solution(4496257250069172487)
XLA Ops:
  56.8 11.2 %all-to-all-start = ((bf16[128,32,128]{2,1,0:T(8,128)(2,1)}), bf16[128,32,128]{2,1,0:T(8,128)(2,1)S(1)}, u32[]{:S(2)}, u32[]{:S(2)}) async-start(bf16[128,32,128]{2,1,0:T(8,128)(2,1)} %bitcast.51), calls=%async_computation | async-start | bytes 2097152 | tf_op jit(solution)/shard_map/all_to_all | solution.py:150
  68.0 19.0 %all-to-all-done = bf16[128,32,128]{2,1,0:T(8,128)(2,1)S(1)} async-done(((bf16[128,32,128]{2,1,0:T(8,128)(2,1)}), bf16[128,32,128]{2,1,0:T(8,128)(2,1)S(1)}, u32[]{:S(2)}, u32[]{:S(2)}) %all-to-all-start) | async-done | bytes 1048608 | tf_op jit(solution)/shard_map/all_to_all | solution.py:150
  87.1 41.1 %while.14 = (s32[]{:T(128)}, bf16[8,512,128]{2,1,0:T(8,128)(2,1)}, bf16[8,512,1]{1,0,2:T(8,128)(2,1)S(1)}, bf16[8,512,1]{1,0,2:T(8,128)(2,1)S(1)}, bf16[8,512,1,...) while((s32[]{:T(128)}, bf16[8,512,128]{2,1,0:T(8,128)(2,1)}, ...), condition=%wide.region_4.5_spmd, body=%wide.region_1.4_spmd.sunk | while | flops 1090650112 | bytes 31745668 | solution.py:61
  128.9 4.6 all-to-all-start.1
  134.3 8.7 %all-to-all-done.1 = bf16[128,32,1]{1,2,0:T(2,128)(2,1)S(1)} async-done(((bf16[128,32,1]{1,2,0:T(2,128)(2,1)}), bf16[128,32,1]{1,2,0:T(2,128)(2,1)S(1)}, u32[]{:S(2)}, u32[]{:S(2)}) %all-to-all-start.1) | async-done | bytes 8224 | tf_op jit(solution)/shard_map/all_to_all | solution.py:161
  142.9 4.6 all-to-all-start.2
  147.6 9.4 %all-to-all-done.2 = bf16[128,32,1]{1,2,0:T(2,128)(2,1)S(1)} async-done(((bf16[128,32,1]{1,2,0:T(2,128)(2,1)}), bf16[128,32,1]{1,2,0:T(2,128)(2,1)S(1)}, u32[]{:S(2)}, u32[]{:S(2)}) %all-to-all-start.2) | async-done | bytes 8224 | tf_op jit(solution)/shard_map/all_to_all | solution.py:162
  157.0 4.8 all-to-all-start.3
  169.9 10.8 %all-to-all-done.3 = bf16[128,32,128]{2,1,0:T(8,128)(2,1)S(1)} async-done(((bf16[128,32,128]{2,1,0:T(8,128)(2,1)}), bf16[128,32,128]{2,1,0:T(8,128)(2,1)S(1)}, u32[]{:S(2)}, u32[]{:S(2)}) %all-to-all-start.3) | async-done | bytes 1048608 | tf_op jit(solution)/shard_map/all_to_all | solution.py:160
  186.9 4.9 dynamic_update_slice.131
  191.8 5.9 %dynamic_update_slice.132 = bf16[160,2048]{0,1:T(8,128)(2,1)S(1)} dynamic-update-slice(bf16[160,2048]{0,1:T(8,128)(2,1)S(1)} %dynamic_update_slice.131, bf16[32,2048]{0,1:T(8,128)(2,1)} %bitcast.379, s32[]{:T(128)S(6)} %select_n.137, s32[]{:T(128)} %constant.96.clone.1) | dynamic-update-slice | bytes 262148 | tf_op jit(solution)/shard_map/dynamic_update_slice | solution.py:185
  197.7 5.9 %dynamic_update_slice.133 = bf16[160,2048]{0,1:T(8,128)(2,1)S(1)} dynamic-update-slice(bf16[160,2048]{0,1:T(8,128)(2,1)S(1)} %dynamic_update_slice.132, bf16[32,2048]{0,1:T(8,128)(2,1)} %bitcast.378, s32[]{:T(128)S(6)} %select_n.140, s32[]{:T(128)} %constant.96.clone.1) | dynamic-update-slice | bytes 262148 | tf_op jit(solution)/shard_map/dynamic_update_slice | solution.py:185
  203.7 5.9 %dynamic_update_slice.134 = bf16[160,2048]{0,1:T(8,128)(2,1)S(1)} dynamic-update-slice(bf16[160,2048]{0,1:T(8,128)(2,1)S(1)} %dynamic_update_slice.133, bf16[32,2048]{0,1:T(8,128)(2,1)} %bitcast.377, s32[]{:T(128)S(6)} %select_n.143, s32[]{:T(128)} %constant.96.clone.1) | dynamic-update-slice | bytes 262148 | tf_op jit(solution)/shard_map/dynamic_update_slice | solution.py:185
  209.6 5.9 %dynamic_update_slice.135 = bf16[160,2048]{0,1:T(8,128)(2,1)S(1)} dynamic-update-slice(bf16[160,2048]{0,1:T(8,128)(2,1)S(1)} %dynamic_update_slice.134, bf16[32,2048]{0,1:T(8,128)(2,1)} %bitcast.376, s32[]{:T(128)S(6)} %select_n.146, s32[]{:T(128)} %constant.96.clone.1) | dynamic-update-slice | bytes 262148 | tf_op jit(solution)/shard_map/dynamic_update_slice | solution.py:185
  215.6 4.0 dynamic_update_slice.136
  223.6 4.2 dynamic_update_slice.138
  233.1 4.3 stack.2
  237.5 4.9 all-to-all-start.4
  245.4 13.2 %all-reduce.1 = bf16[512]{0:T(512)(128)(2,1)S(1)} all-reduce(bf16[512]{0:T(512)(128)(2,1)S(1)} %dynamic-update-slice), channel_id=1, replica_groups=mesh['grp'=8,'dev'=16] {'grp'}, use_global_device_ids=true, to_apply=%add.1 | all-reduce | flops 512 | bytes 2048
  258.6 11.0 %all-gather.3.cloned.1.call-done = bf16[2048,512]{0,1:T(8,128)(2,1)} async-done(((bf16[2048,64]{0,1:T(8,128)(2,1)}), bf16[2048,512]{0,1:T(8,128)(2,1)}) %all-gather.3.cloned.1.call-update) | async-done | bytes 2097168 | tf_op jit(solution)/shard_map/all_gather | solution.py:203
  269.7 27.4 %all-gather.5.cloned.1.call-done = bf16[512,2048]{1,0:T(8,128)(2,1)} async-done(((bf16[64,2048]{1,0:T(8,128)(2,1)}), bf16[512,2048]{1,0:T(8,128)(2,1)}) %all-gather.5.cloned.1.call-update) | async-done | bytes 2097168 | tf_op jit(solution)/shard_map/all_gather | solution.py:205
  297.1 85.8 %all-to-all-done.4 = bf16[16,128,2048]{2,1,0:T(8,128)(2,1)} async-done(((bf16[16,128,2048]{2,1,0:T(8,128)(2,1)}), bf16[16,128,2048]{2,1,0:T(8,128)(2,1)}, u32[]{:S(2)}, u32[]{:S(2)}) %all-to-all-start.4) | async-done | bytes 8388640 | tf_op jit(solution)/shard_map/all_to_all | solution.py:209
  382.8 15.2 %convolution_convert_fusion = bf16[2048,2048]{1,0:T(8,128)(2,1)} fusion(bf16[512,2048]{1,0:T(8,128)(2,1)} %all-gather.5.cloned.1.call-done, bf16[2048,2048]{1,0:T(8,128)(2,1)} %bitcast.138, bf16[2048,512]{0,1:T(8,128)(2,1)} %all-gather.3.cloned.1.call-done, f32[512]{0:T(512)S(1)} %convert_element_type.97), kind=kOutput, calls=%fused_computation.17 | convolution fusion | flops 8604614656 | bytes 20973568 | tf_op jit(solution)/shard_map/dot_general | solution.py:215
  398.1 92.4 %reduce-scatter.2.cloned.1.call-done = bf16[128,2048]{1,0:T(8,128)(2,1)} async-done(((bf16[2048,2048]{1,0:T(8,128)(2,1)}), bf16[128,2048]{1,0:T(8,128)(2,1)}) %reduce-scatter.2.cloned.1.call-update) | async-done | bytes 524304 | tf_op jit(solution)/shard_map/reduce_scatter | solution.py:214
  (213 shorter events, 92.9 us)
Async XLA Ops:
  6.5 157.5 %copy-start = (bf16[128,2048]{1,0:T(8,128)(2,1)S(1)}, bf16[128,2048]{1,0:T(8,128)(2,1)}, u32[]{:S(2)}) copy-start(bf16[128,2048]{1,0:T(8,128)(2,1)} %param.19) | copy-start | bytes 1572868
  6.5 80.5 %copy-start.1 = (bf16[1,4096,128]{2,1,0:T(8,128)(2,1)S(1)}, bf16[1,4096,128]{2,1,0:T(8,128)(2,1)}, u32[]{:S(2)}) copy-start(bf16[1,4096,128]{2,1,0:T(8,128)(2,1)} %param.24) | copy-start | bytes 3145732
  56.8 30.3 %all-to-all-start = ((bf16[128,32,128]{2,1,0:T(8,128)(2,1)}), bf16[128,32,128]{2,1,0:T(8,128)(2,1)S(1)}, u32[]{:S(2)}, u32[]{:S(2)}) async-start(bf16[128,32,128]{2,1,0:T(8,128)(2,1)} %bitcast.51), calls=%async_computation | async-start | bytes 2097152 | tf_op jit(solution)/shard_map/all_to_all | solution.py:150
  87.1 60.5 %copy-start.6 = (s32[1,8]{1,0:T(1,128)S(1)}, s32[1,8]{1,0:T(1,128)}, u32[]{:S(2)}) copy-start(s32[1,8]{1,0:T(1,128)} %param.22) | copy-start | bytes 100
  87.1 77.0 %copy-start.3 = (bf16[128,2048]{1,0:T(8,128)(2,1)S(1)}, bf16[128,2048]{1,0:T(8,128)(2,1)}, u32[]{:S(2)}) copy-start(bf16[128,2048]{1,0:T(8,128)(2,1)} %param.18) | copy-start | bytes 1572868
  98.7 1.5 copy-start.11
  109.0 1.5 copy-start.11
  119.3 1.5 copy-start.11
  124.4 1.5 copy-start.11
  128.9 14.0 %all-to-all-start.1 = ((bf16[128,32,1]{1,2,0:T(2,128)(2,1)}), bf16[128,32,1]{1,2,0:T(2,128)(2,1)S(1)}, u32[]{:S(2)}, u32[]{:S(2)}) async-start(bf16[128,32,1]{1,2,0:T(2,128)(2,1)} %reshape.406), calls=%async_computation.1 | async-start | bytes 131072 | tf_op jit(solution)/shard_map/all_to_all | solution.py:161
  142.9 14.1 %all-to-all-start.2 = ((bf16[128,32,1]{1,2,0:T(2,128)(2,1)}), bf16[128,32,1]{1,2,0:T(2,128)(2,1)S(1)}, u32[]{:S(2)}, u32[]{:S(2)}) async-start(bf16[128,32,1]{1,2,0:T(2,128)(2,1)} %reshape.407), calls=%async_computation.2 | async-start | bytes 131072 | tf_op jit(solution)/shard_map/all_to_all | solution.py:162
  157.0 23.7 %all-to-all-start.3 = ((bf16[128,32,128]{2,1,0:T(8,128)(2,1)}), bf16[128,32,128]{2,1,0:T(8,128)(2,1)S(1)}, u32[]{:S(2)}, u32[]{:S(2)}) async-start(bf16[128,32,128]{2,1,0:T(8,128)(2,1)} %bitcast.381), calls=%async_computation.3 | async-start | bytes 2097152 | tf_op jit(solution)/shard_map/all_to_all | solution.py:160
  227.9 4.4 copy-start.2
  227.9 4.9 copy-start.7
  227.9 4.9 copy-start.8
  237.4 6.4 %copy-start.13 = (u32[128]{0:T(128)S(1)}, u32[128]{0:T(128)}, u32[]{:S(2)}) copy-start(u32[128]{0:T(128)} %constant.119) | copy-start | bytes 1540
  237.4 7.7 %copy-start.12 = (bf16[64]{0:T(256)(128)(2,1)S(1)}, bf16[64]{0:T(256)(128)(2,1)}, u32[]{:S(2)}) copy-start(bf16[64]{0:T(256)(128)(2,1)} %param.27) | copy-start | bytes 388
  237.5 145.4 %all-to-all-start.4 = ((bf16[16,128,2048]{2,1,0:T(8,128)(2,1)}), bf16[16,128,2048]{2,1,0:T(8,128)(2,1)}, u32[]{:S(2)}, u32[]{:S(2)}) async-start(bf16[16,128,2048]{2,1,0:T(8,128)(2,1)} %stack.2), calls=%async_computation.4 | async-start | bytes 16777216 | tf_op jit(solution)/shard_map/all_to_all | solution.py:209
  242.3 27.3 %all-gather.3.cloned.1.call-start = ((), (), s32[]{:S(2)}) async-start(), calls=%async_computation.6 | async-start | bytes 2359296 | tf_op jit(solution)/shard_map/all_gather | solution.py:203
  243.1 54.0 %all-gather.5.cloned.1.call-start = ((), (), s32[]{:S(2)}) async-start(), calls=%async_computation.7 | async-start | bytes 2359296 | tf_op jit(solution)/shard_map/all_gather | solution.py:205
  243.8 246.6 %reduce-scatter.2.cloned.1.call-start = ((), (), s32[]{:S(2)}) async-start(), calls=%async_computation.8 | async-start | bytes 8912896 | tf_op jit(solution)/shard_map/reduce_scatter | solution.py:214
  398.0 92.4 %copy-start.5 = (f32[2048]{0:T(1024)S(1)}, f32[2048]{0:T(1024)}, u32[]{:S(2)}) copy-start(f32[2048]{0:T(1024)} %param.29) | copy-start | bytes 24580
  398.0 95.1 %copy-start.9 = (f32[2048]{0:T(1024)S(1)}, f32[2048]{0:T(1024)}, u32[]{:S(2)}) copy-start(f32[2048]{0:T(1024)} %param.33) | copy-start | bytes 24580
  398.0 95.1 %copy-start.10 = (f32[2048]{0:T(1024)S(1)}, f32[2048]{0:T(1024)}, u32[]{:S(2)}) copy-start(f32[2048]{0:T(1024)} %param.32) | copy-start | bytes 24580
  (5 other events, 7.0 us)
Sparse Core Ops, SparseCore 0:
  244.9 24.7 all-gather.2
  271.4 25.6 all-gather.4
  398.2 92.2 reduce-scatter.1
